TPU v7x, 32 devices: a whole 2x2x4 slice. The times are simulated.
32 devices in a mesh: rep: 2 (over x), shard: 16 (over z, y, core).
Axes of the slice: x: 2, y: 2, z: 4, core: 2. Of those that a mesh axis runs over, the one named last changes fastest.
Arguments:
- block_input: bfloat16 [4096, 2048], P(('rep', 'shard')), may hold values from -6 to 6
- out_grad: bfloat16 [4096, 2048], P(('rep', 'shard')), may hold values from -6 to 6
- segments: int32 [32, 128], P(('rep', 'shard')), may hold values from 0 to 2, as said below
- positions: int32 [32, 128], P(('rep', 'shard')), may hold values from 0 to 1023, as said below
- attn_gain: float32 [2048], replicated, may hold values from 0.5 to 1.5
- mlp_gain: float32 [2048], replicated, may hold values from 0.5 to 1.5
- q_gain: float32 [128], replicated, may hold values from 0.5 to 2
- k_gain: float32 [128], replicated, may hold values from 0.5 to 2
- w_q: bfloat16 [2048, 2048], P('shard'), may hold values from -0.125 to 0.125
- key_matrix: bfloat16 [2048, 1024], P('shard'), may hold values from -0.125 to 0.125
- value_matrix: bfloat16 [2048, 1024], P('shard'), may hold values from -0.125 to 0.125
- w_o: bfloat16 [2048, 2048], P('shard'), may hold values from -0.75 to 0.75
- w_gate: bfloat16 [2048, 6144], P('shard'), may hold values from -0.125 to 0.125
- w_up: bfloat16 [2048, 6144], P('shard'), may hold values from -0.125 to 0.125
- w_down: bfloat16 [2048, 6144], P('shard'), may hold values from -0.078125 to 0.078125
Outputs:
- output: bfloat16 [4096, 2048], P(('rep', 'shard'))
- grad_input: float32 [4096, 2048], P(('rep', 'shard'))
- grad_w_q: float32 [2048, 2048], P('shard')
- grad_w_k: float32 [2048, 1024], P('shard')
- grad_w_v: float32 [2048, 1024], P('shard')
- grad_w_o: float32 [2048, 2048], P('shard')
- grad_w_gate: float32 [2048, 6144], P('shard')
- grad_w_up: float32 [2048, 6144], P('shard')
- grad_w_down: float32 [2048, 6144], P('shard')
- grad_attn_gain: float32 [2048], replicated
- grad_mlp_gain: float32 [2048], replicated
- grad_q_gain: float32 [128], replicated
- grad_k_gain: float32 [128], replicated
Inputs may be any that keep to these rules, and one draw needn't show every extreme that they name: `segments`: in each sequence the segment numbers never fall, the first token has 0 and the last has 2. Within a segment the positions rise by one from token to token; segments 1 and 2 start at position 0.
All inputs are finite; a program needn't handle non-finite values.
Results may differ from a plain program's by a relative error of at most 0.015.
Values may be sent and summed in bfloat16 or wider, within the bound.
No kernel may reach another device: no remote copies, remote signals or barrier semaphores. Data moves between devices by JAX's collectives and lax.ppermute only.
A program may use at most 768 MiB of HBM per device.

v0:
```python
import math
import jax
import jax.numpy as jnp
from jax import lax
from jax.sharding import PartitionSpec as P

EPSILON = 1e-06
ROPE_BASE = 1000000.0
NEG_FILL = -1e30


def rope_tables(positions, half):
    freq = jnp.exp(jnp.arange(half, dtype=jnp.float32) * (-math.log(ROPE_BASE) / half))
    angles = positions.reshape(-1).astype(jnp.float32)[:, None, None] * freq
    return (jnp.cos(angles), jnp.sin(angles))


def rotate(vectors, cosine, sine):
    half = vectors.shape[-1] // 2
    first, second = (vectors[..., :half], vectors[..., half:])
    return jnp.concatenate([first * cosine - second * sine, second * cosine + first * sine], -1)


def unrotate(grads, cosine, sine):
    half = grads.shape[-1] // 2
    first, second = (grads[..., :half], grads[..., half:])
    return jnp.concatenate([first * cosine + second * sine, second * cosine - first * sine], -1)


def head_norm(heads, gain):
    recip = lax.rsqrt(jnp.mean(heads * heads, -1, keepdims=True) + EPSILON)
    return (heads * recip * gain, recip)


def norm_back(grads, inputs, recip, gain, axes):
    normal = inputs * recip
    scaled = grads * gain
    gain_grad = jnp.sum(grads * normal, axis=axes)
    input_grad = recip * (scaled - normal * jnp.mean(scaled * normal, -1, keepdims=True))
    return (input_grad, gain_grad)


def attention_mask(segments):
    packed_length = segments.shape[1]
    same = segments[:, :, None] == segments[:, None, :]
    places = jnp.arange(packed_length)
    causal = places[None, :] <= places[:, None]
    return same & causal[None]


def contract_rows(left, right):
    return lax.dot_general(
        left, right, (((0,), (0,)), ((), ())), preferred_element_type=jnp.float32
    )


def contract_cols(left, right):
    return lax.dot_general(
        left, right, (((1,), (1,)), ((), ())), preferred_element_type=jnp.float32
    )


def head_scores(rotated_query_rows, rotated_key_rows, mask, kv_heads, head):
    sequence_list, packed_length = (mask.shape[0], mask.shape[1])
    groups = rotated_query_rows.shape[1] // kv_heads
    query_rows = rotated_query_rows.reshape(sequence_list, packed_length, kv_heads, groups, head)
    every_key_row = rotated_key_rows.reshape(sequence_list, packed_length, kv_heads, head)
    scores = jnp.einsum(
        "slkgd,smkd->skglm", query_rows, every_key_row, preferred_element_type=jnp.float32
    ) * head ** (-0.5)
    return (jnp.where(mask[:, None, None], scores, NEG_FILL), query_rows, every_key_row)


def attend_forward(rotated_query_rows, rotated_key_rows, value_rows, mask):
    sequence_list, packed_length = (mask.shape[0], mask.shape[1])
    kv_heads, head = (value_rows.shape[1], value_rows.shape[2])
    scores, query_rows, every_key_row = head_scores(
        rotated_query_rows, rotated_key_rows, mask, kv_heads, head
    )
    top = jnp.max(scores, -1, keepdims=True)
    expo = jnp.exp(scores - top)
    total = jnp.sum(expo, -1, keepdims=True)
    probs = (expo / total).astype(jnp.bfloat16)
    log_total = top + jnp.log(total)
    value_heads = value_rows.reshape(sequence_list, packed_length, kv_heads, head)
    attended_rows = jnp.einsum(
        "skglm,smkd->slkgd", probs, value_heads, preferred_element_type=jnp.float32
    )
    return (
        attended_rows.reshape(
            sequence_list * packed_length, rotated_query_rows.shape[1] * head
        ).astype(jnp.bfloat16),
        log_total,
    )


def attend_backward(
    rotated_query_rows,
    rotated_key_rows,
    value_rows,
    attended_rows,
    attended_gradient,
    log_total,
    mask,
):
    sequence_list, packed_length = (mask.shape[0], mask.shape[1])
    kv_heads, head = (value_rows.shape[1], value_rows.shape[2])
    groups = rotated_query_rows.shape[1] // kv_heads
    scores, query_rows, every_key_row = head_scores(
        rotated_query_rows, rotated_key_rows, mask, kv_heads, head
    )
    probs_back = jnp.where(mask[:, None, None], jnp.exp(scores - log_total), 0.0)
    output_gradient = attended_gradient.reshape(
        sequence_list, packed_length, kv_heads, groups, head
    )
    value_heads = value_rows.reshape(sequence_list, packed_length, kv_heads, head)
    value_rows_gradient = jnp.einsum(
        "skglm,slkgd->smkd",
        probs_back.astype(jnp.bfloat16),
        output_gradient,
        preferred_element_type=jnp.float32,
    )
    grad_probs = jnp.einsum(
        "slkgd,smkd->skglm", output_gradient, value_heads, preferred_element_type=jnp.float32
    )
    complete_output = attended_rows.reshape(
        sequence_list, packed_length, kv_heads, groups, head
    ).astype(jnp.float32)
    delta = jnp.transpose(
        jnp.sum(output_gradient.astype(jnp.float32) * complete_output, -1), (0, 2, 3, 1)
    )[..., None]
    grad_scores = (probs_back * (grad_probs - delta)).astype(jnp.bfloat16)
    rotated_query_gradient = jnp.einsum(
        "skglm,smkd->slkgd", grad_scores, every_key_row, preferred_element_type=jnp.float32
    ) * head ** (-0.5)
    rotated_key_gradient = jnp.einsum(
        "skglm,slkgd->smkd", grad_scores, query_rows, preferred_element_type=jnp.float32
    ) * head ** (-0.5)
    token_rows = sequence_list * packed_length
    return (
        rotated_query_gradient.reshape(token_rows, rotated_query_rows.shape[1], head),
        rotated_key_gradient.reshape(token_rows, kv_heads, head),
        value_rows_gradient.reshape(token_rows, kv_heads, head),
    )


def on_device(
    block_input,
    out_grad,
    segments,
    positions,
    attn_gain,
    mlp_gain,
    q_gain,
    k_gain,
    w_q,
    key_matrix,
    value_matrix,
    w_o,
    w_gate,
    w_up,
    w_down,
):
    tokens, width = block_input.shape
    head = q_gain.shape[0]
    heads = w_q.shape[1] // head
    kv_heads = key_matrix.shape[1] // head
    hidden = w_gate.shape[1]
    mask = attention_mask(segments)
    cosine, sine = rope_tables(positions, head // 2)
    inputs = block_input.astype(jnp.float32)
    recip_attn = lax.rsqrt(jnp.mean(inputs * inputs, -1, keepdims=True) + EPSILON)
    normed_rows = (inputs * recip_attn * attn_gain).astype(jnp.bfloat16)
    pieces = (
        lax.all_gather(w_q, "shard", axis=0, tiled=True),
        lax.all_gather(key_matrix, "shard", axis=0, tiled=True),
        lax.all_gather(value_matrix, "shard", axis=0, tiled=True),
    )
    columns = normed_rows
    q_proj, k_proj, v_proj = tuple(
        (
            jnp.dot(columns, weight_piece, preferred_element_type=jnp.float32)
            for weight_piece in pieces
        )
    )
    q_heads = q_proj.reshape(tokens, heads, head)
    key_head_rows = k_proj.reshape(tokens, kv_heads, head)
    q_normed, q_recip = head_norm(q_heads, q_gain)
    k_normed, k_recip = head_norm(key_head_rows, k_gain)
    rotated_query_rows = rotate(q_normed, cosine, sine).astype(jnp.bfloat16)
    rotated_key_rows = rotate(k_normed, cosine, sine).astype(jnp.bfloat16)
    value_rows = v_proj.astype(jnp.bfloat16).reshape(tokens, kv_heads, head)
    attended_rows, log_total = attend_forward(
        rotated_query_rows, rotated_key_rows, value_rows, mask
    )
    attn_out = contract_cols(attended_rows, lax.all_gather(w_o, "shard", axis=0, tiled=True))
    mid = inputs + attn_out
    recip_mlp = lax.rsqrt(jnp.mean(mid * mid, -1, keepdims=True) + EPSILON)
    mlp_in = (mid * recip_mlp * mlp_gain).astype(jnp.bfloat16)
    pieces = (
        lax.all_gather(w_gate, "shard", axis=0, tiled=True),
        lax.all_gather(w_up, "shard", axis=0, tiled=True),
    )
    columns = mlp_in
    gate_pre = jnp.dot(columns, pieces[0], preferred_element_type=jnp.float32)
    up_pre = jnp.dot(columns, pieces[1], preferred_element_type=jnp.float32)
    sigma = jax.nn.sigmoid(gate_pre)
    silu_gate = gate_pre * sigma
    act = (silu_gate * up_pre).astype(jnp.bfloat16)
    mlp_out = contract_cols(act, lax.all_gather(w_down, "shard", axis=0, tiled=True))
    output = (mid + mlp_out).astype(jnp.bfloat16)
    grad_top = out_grad.astype(jnp.float32)
    columns = out_grad
    grad_act = jnp.dot(
        columns,
        lax.all_gather(w_down, "shard", axis=0, tiled=True),
        preferred_element_type=jnp.float32,
    )
    grad_gate = (grad_act * up_pre * sigma * (1.0 + gate_pre * (1.0 - sigma))).astype(jnp.bfloat16)
    grad_up = (grad_act * silu_gate).astype(jnp.bfloat16)
    pieces = (
        lax.all_gather(w_gate, "shard", axis=0, tiled=True),
        lax.all_gather(w_up, "shard", axis=0, tiled=True),
    )
    part = contract_cols(grad_gate, pieces[0]) + contract_cols(grad_up, pieces[1])
    grad_mlp_in = part
    mlp_right = jnp.concatenate([grad_gate, grad_up], 1)
    left_in = mlp_in
    left_grad = out_grad
    mlp_grads = lax.psum_scatter(
        jnp.concatenate([contract_rows(left_in, mlp_right), contract_rows(left_grad, act)], 1),
        "shard",
        scatter_dimension=0,
        tiled=True,
    )
    grad_mid_part, mlp_gain_part = norm_back(grad_mlp_in, mid, recip_mlp, mlp_gain, 0)
    grad_mid = grad_top + grad_mid_part
    grad_mid_b = grad_mid.astype(jnp.bfloat16)
    columns = grad_mid_b
    attended_gradient = jnp.dot(
        columns,
        lax.all_gather(w_o, "shard", axis=0, tiled=True),
        preferred_element_type=jnp.float32,
    ).astype(jnp.bfloat16)
    rotated_query_gradient, rotated_key_gradient, value_rows_gradient = attend_backward(
        rotated_query_rows,
        rotated_key_rows,
        value_rows,
        attended_rows,
        attended_gradient,
        log_total,
        mask,
    )
    grad_qh, q_gain_part = norm_back(
        unrotate(rotated_query_gradient, cosine, sine), q_heads, q_recip, q_gain, (0, 1)
    )
    key_heads_gradient, k_gain_part = norm_back(
        unrotate(rotated_key_gradient, cosine, sine), key_head_rows, k_recip, k_gain, (0, 1)
    )
    grad_q = grad_qh.reshape(tokens, heads * head).astype(jnp.bfloat16)
    key_gradient = key_heads_gradient.reshape(tokens, kv_heads * head).astype(jnp.bfloat16)
    value_gradient = value_rows_gradient.reshape(tokens, kv_heads * head).astype(jnp.bfloat16)
    pieces = (
        lax.all_gather(w_q, "shard", axis=0, tiled=True),
        lax.all_gather(key_matrix, "shard", axis=0, tiled=True),
        lax.all_gather(value_matrix, "shard", axis=0, tiled=True),
    )
    part = (
        contract_cols(grad_q, pieces[0])
        + contract_cols(key_gradient, pieces[1])
        + contract_cols(value_gradient, pieces[2])
    )
    attn_right = jnp.concatenate([grad_q, key_gradient, value_gradient], 1)
    left_in = normed_rows
    left_grad = grad_mid_b
    attn_grads = lax.psum_scatter(
        jnp.concatenate(
            [contract_rows(left_in, attn_right), contract_rows(left_grad, attended_rows)], 1
        ),
        "shard",
        scatter_dimension=0,
        tiled=True,
    )
    grad_in_part, attn_gain_part = norm_back(part, inputs, recip_attn, attn_gain, 0)
    grad_input = grad_mid + grad_in_part
    gain_totals = lax.psum(
        (attn_gain_part, mlp_gain_part, q_gain_part, k_gain_part), ("rep", "shard")
    )
    attn_total, mlp_total = (
        lax.psum(attn_grads.astype(jnp.bfloat16), "rep").astype(jnp.float32),
        lax.psum(mlp_grads.astype(jnp.bfloat16), "rep").astype(jnp.float32),
    )
    q_cols = heads * head
    k_cols = kv_heads * head
    grad_w_q = attn_total[:, :q_cols]
    grad_w_k = attn_total[:, q_cols : q_cols + k_cols]
    grad_w_v = attn_total[:, q_cols + k_cols : q_cols + 2 * k_cols]
    grad_w_o = attn_total[:, q_cols + 2 * k_cols :]
    grad_w_gate = mlp_total[:, :hidden]
    grad_w_up = mlp_total[:, hidden : 2 * hidden]
    grad_w_down = mlp_total[:, 2 * hidden :]
    return (
        output,
        grad_input,
        grad_w_q,
        grad_w_k,
        grad_w_v,
        grad_w_o,
        grad_w_gate,
        grad_w_up,
        grad_w_down,
        gain_totals[0],
        gain_totals[1],
        gain_totals[2],
        gain_totals[3],
    )


def solution(mesh):
    placed = (
        P(("rep", "shard"), None),
        P(("rep", "shard"), None),
        P(("rep", "shard"), None),
        P(("rep", "shard"), None),
        P(),
        P(),
        P(),
        P(),
        P("shard", None),
        P("shard", None),
        P("shard", None),
        P("shard", None),
        P("shard", None),
        P("shard", None),
        P("shard", None),
    )
    return jax.shard_map(
        on_device,
        mesh=mesh,
        in_specs=placed,
        out_specs=(
            P(("rep", "shard"), None),
            P(("rep", "shard"), None),
            P("shard", None),
            P("shard", None),
            P("shard", None),
            P("shard", None),
            P("shard", None),
            P("shard", None),
            P("shard", None),
            P(),
            P(),
            P(),
            P(),
        ),
        check_vma=False,
    )
```

profile of v0, /device:TPU:0, one launch (start us, length us, event | category | flops | bytes accessed | tf_op | source)
XLA Modules:
  0.0 2806.3 jit_solution(15419628978582923309)
XLA Ops:
  7.3 0.7 all-gather.8.cloned.1.call-update
  8.0 0.7 all-gather.10.cloned.1.call-update
  8.8 0.7 all-gather.12.cloned.1.call-update
  11.3 0.7 all-gather.20.cloned.1.call-update
  13.5 0.7 fusion.56
  14.5 49.1 %all-gather.8.cloned.1.call-done = bf16[2048,1024]{1,0:T(8,128)(2,1)} async-done(((bf16[128,1024]{1,0:T(8,128)(2,1)}), bf16[2048,1024]{1,0:T(8,128)(2,1)}) %all-gather.8.cloned.1.call-update) | async-done | bytes 4194320 | tf_op jit(solution)/shard_map/all_gather | solution.py:177
  63.5 2.9 fusion.19
  66.6 48.2 %all-gather.10.cloned.1.call-done = bf16[2048,1024]{1,0:T(8,128)(2,1)} async-done(((bf16[128,1024]{1,0:T(8,128)(2,1)}), bf16[2048,1024]{1,0:T(8,128)(2,1)}) %all-gather.10.cloned.1.call-update) | async-done | bytes 4194320 | tf_op jit(solution)/shard_map/all_gather | solution.py:176
  114.8 2.9 fusion.66
  118.1 0.8 copy.171
  119.3 71.0 %all-gather.12.cloned.1.call-done = bf16[2048,2048]{1,0:T(8,128)(2,1)} async-done(((bf16[128,2048]{1,0:T(8,128)(2,1)}), bf16[2048,2048]{1,0:T(8,128)(2,1)}) %all-gather.12.cloned.1.call-update) | async-done | bytes 8388624 | tf_op jit(solution)/shard_map/all_gather | solution.py:175
  190.4 4.7 fusion.64
  199.0 0.8 copy-done.9
  200.2 65.4 %all-gather.14.cloned.1.call-done = bf16[2048,2048]{1,0:T(8,128)(2,1)} async-done(((bf16[128,2048]{1,0:T(8,128)(2,1)}), bf16[2048,2048]{1,0:T(8,128)(2,1)}) %all-gather.14.cloned.1.call-update) | async-done | bytes 8388624 | tf_op jit(solution)/shard_map/all_gather | solution.py:196
  265.6 6.4 multiply_reduce_fusion.4
  272.0 0.7 log_add_fusion
  272.8 121.1 %all-gather.18.cloned.1.call-done = bf16[2048,6144]{1,0:T(8,128)(2,1)} async-done(((bf16[128,6144]{1,0:T(8,128)(2,1)}), bf16[2048,6144]{1,0:T(8,128)(2,1)}) %all-gather.18.cloned.1.call-update) | async-done | bytes 25165840 | tf_op jit(solution)/shard_map/all_gather | solution.py:202
  393.9 13.7 fusion.75
  407.6 116.4 %all-gather.16.cloned.1.call-done = bf16[2048,6144]{1,0:T(8,128)(2,1)} async-done(((bf16[128,6144]{1,0:T(8,128)(2,1)}), bf16[2048,6144]{1,0:T(8,128)(2,1)}) %all-gather.16.cloned.1.call-update) | async-done | bytes 25165840 | tf_op jit(solution)/shard_map/all_gather | solution.py:201
  524.0 13.2 fusion.74
  537.2 117.0 %all-gather.20.cloned.1.call-done = bf16[2048,6144]{1,0:T(8,128)(2,1)} async-done(((bf16[128,6144]{1,0:T(8,128)(2,1)}), bf16[2048,6144]{1,0:T(8,128)(2,1)}) %all-gather.20.cloned.1.call-update) | async-done | bytes 25165840 | tf_op jit(solution)/shard_map/all_gather | solution.py:210
  654.2 14.8 multiply_convert_fusion
  668.9 13.5 fusion.76
  682.5 15.2 multiply_reduce_fusion
  697.7 0.7 broadcast_multiply_fusion.3
  698.3 1.7 multiply_add_fusion.1
  700.0 5.8 convolution_convert_fusion
  705.8 2.1 copy.172
  708.0 2.2 copy.132
  710.2 1.6 multiply_reduce_fusion.2
  711.8 2.1 fusion.18
  713.9 1.5 fusion.15
  715.9 1.5 convolution_multiply_fusion
  717.4 8.1 fusion.50
  725.7 2.1 fusion.72
  728.6 1.1 fusion.55
  729.8 0.7 copy.142
  730.5 2.4 copy.169
  732.9 1.5 multiply_add_fusion
  734.5 1.7 multiply_reduce_fusion.1
  736.7 0.9 fusion.44
  738.3 2.2 fusion.30
  740.5 13.6 fusion.31
  754.1 33.6 %pad_maximum_fusion.1 = f32[2048,6144]{1,0:T(8,128)} fusion(f32[2048,2048]{1,0:T(8,128)} %fusion.50, f32[2048,4096]{1,0:T(8,128)} %fusion.31), kind=kLoop, calls=%fused_computation.1 | loop fusion | flops 12582912 | bytes 100663296 | tf_op jit(solution)/shard_map/concatenate | solution.py:277
  787.8 1.3 copy-done.13
  789.1 32.8 %convolution_bitcast_fusion = f32[2048,6144]{1,0:T(8,128)} fusion(bf16[128,6144]{1,0:T(8,128)(2,1)S(1)} %copy-done.13, bf16[128,2048]{1,0:T(8,128)(2,1)} %param.16), kind=kOutput, calls=%fused_computation.2 | convolution fusion | flops 3221225472 | bytes 52428800 | tf_op jit(solution)/shard_map/dot_general | solution.py:52
  822.0 48.1 %fusion = f32[2048,12288]{1,0:T(8,128)} fusion(bf16[128,2048]{1,0:T(8,128)(2,1)} %copy-done.15, bf16[128,6144]{1,0:T(8,128)(2,1)} %get-tuple-element.25, bf16[128,6144]{1,0:T(8,128)(2,1)S(1)} %copy-done.14), kind=kOutput, calls=%fused_computation.3 | convolution fusion | flops 6448742400 | bytes 104333312 | tf_op jit(solution)/shard_map/dot_general | solution.py:52
  870.1 100.2 %pad_maximum_fusion = f32[2048,18432]{1,0:T(8,128)} fusion(f32[2048,6144]{1,0:T(8,128)} %convolution_bitcast_fusion, f32[2048,12288]{1,0:T(8,128)} %fusion), kind=kLoop, calls=%fused_computation | loop fusion | flops 37748736 | bytes 301989888 | tf_op jit(solution)/shard_map/concatenate | solution.py:231
  970.6 285.1 %reduce-scatter.3.cloned.1.call-done = f32[128,6144]{1,0:T(8,128)} async-done(((f32[2048,6144]{1,0:T(8,128)}), f32[128,6144]{1,0:T(8,128)}) %reduce-scatter.3.cloned.1.call-update) | async-done | bytes 3145744 | tf_op jit(solution)/shard_map/reduce_scatter | solution.py:276
  1255.7 3.2 convert_element_type.156
  1258.9 1370.2 %reduce-scatter.5.cloned.1.call-done = f32[128,18432]{1,0:T(8,128)} async-done(((f32[2048,18432]{1,0:T(8,128)}), f32[128,18432]{1,0:T(8,128)}) %reduce-scatter.5.cloned.1.call-update) | async-done | bytes 9437200 | tf_op jit(solution)/shard_map/reduce_scatter | solution.py:230
  2629.1 6.5 convert_element_type.158
  2635.7 0.7 copy-done.53
  2636.7 6.4 fusion.77
  2643.2 1.5 convolution_add_fusion.1
  2644.7 0.8 copy-done.11
  2645.6 2.7 fusion.25
  2648.2 40.2 %all-reduce = (f32[2048]{0:T(1024)}, f32[2048]{0:T(1024)}, f32[128]{0:T(128)}, f32[128]{0:T(128)}) all-reduce(f32[2048]{0:T(1024)S(1)} %get-tuple-element.15, f32[2048]{0:T(1024)S(1)} %copy-done.50, f32[128]{0:T(128)S(1)} %bitcast_reduce_fusion, f32[128]{0:T(128)S(1)} %bitcast_reduce_fusion.1), channel_id=1, replica_groups=mesh['rep'=2,'shard'=16] {'rep','shard'}, use_global_device_ids=true, to_apply=%region_16.17 | all-reduce | flops 4352 | bytes 34816 | tf_op jit(solution)/shard_map/psum | solution.py:286
  2688.5 2.6 fusion.24
  2691.0 14.2 fusion.5
  2705.2 84.7 %all-reduce.4.cloned.1.call-done = (bf16[128,6144]{1,0:T(8,128)(2,1)}, bf16[128,18432]{1,0:T(8,128)(2,1)}) async-done(((bf16[128,6144]{1,0:T(8,128)(2,1)}, bf16[128,18432]{1,0:T(8,128)(2,1)}), (bf16[128,6144]{1,0:T(8,128)(2,1)}, bf16[128,18432]{1,0:T(8,128)(2,1)})) %all-reduce.4.cloned.1.call-update) | async-done | bytes 6291472 | tf_op jit(solution)/shard_map/psum | solution.py:290
  2790.0 2.3 fusion.71
  2792.2 2.8 fusion.70
  2795.0 4.0 fusion.69
  (171 shorter events, 12.2 us)
Async XLA Ops:
  7.2 4.8 copy-start
  7.2 5.0 copy-start.59
  7.2 5.0 copy-start.55
  7.2 5.6 copy-start.57
  7.2 6.2 copy-start.58
  7.2 56.3 %copy-start.37 = (f32[2048]{0:T(1024)S(1)}, f32[2048]{0:T(1024)}, u32[]{:S(2)}) copy-start(f32[2048]{0:T(1024)} %param.19) | copy-start | bytes 24580
  7.2 56.3 %all-gather.8.cloned.1.call-start = ((), (), s32[]{:S(2)}) async-start(), calls=%async_computation.2 | async-start | bytes 4456448 | tf_op jit(solution)/shard_map/all_gather | solution.py:177
  8.0 106.8 %all-gather.10.cloned.1.call-start = ((), (), s32[]{:S(2)}) async-start(), calls=%async_computation.3 | async-start | bytes 4456448 | tf_op jit(solution)/shard_map/all_gather | solution.py:176
  8.7 181.6 %all-gather.12.cloned.1.call-start = ((), (), s32[]{:S(2)}) async-start(), calls=%async_computation.4 | async-start | bytes 8912896 | tf_op jit(solution)/shard_map/all_gather | solution.py:175
  9.5 256.1 %all-gather.14.cloned.1.call-start = ((), (), s32[]{:S(2)}) async-start(), calls=%async_computation.5 | async-start | bytes 8912896 | tf_op jit(solution)/shard_map/all_gather | solution.py:196
  10.0 383.8 %all-gather.18.cloned.1.call-start = ((), (), s32[]{:S(2)}) async-start(), calls=%async_computation.7 | async-start | bytes 26738688 | tf_op jit(solution)/shard_map/all_gather | solution.py:202
  10.6 513.3 %all-gather.16.cloned.1.call-start = ((), (), s32[]{:S(2)}) async-start(), calls=%async_computation.6 | async-start | bytes 26738688 | tf_op jit(solution)/shard_map/all_gather | solution.py:201
  11.2 643.0 %all-gather.20.cloned.1.call-start = ((), (), s32[]{:S(2)}) async-start(), calls=%async_computation.8 | async-start | bytes 26738688 | tf_op jit(solution)/shard_map/all_gather | solution.py:210
  12.0 1243.7 %reduce-scatter.3.cloned.1.call-start = ((), (), s32[]{:S(2)}) async-start(), calls=%async_computation.9 | async-start | bytes 53477376 | tf_op jit(solution)/shard_map/reduce_scatter | solution.py:276
  12.2 178.1 %copy-start.46 = (f32[128]{0:T(128)}, f32[128]{0:T(128)S(1)}, u32[]{:S(2)}) copy-start(f32[128]{0:T(128)S(1)} %add_rsqrt_fusion.3) | copy-start | bytes 1540
  66.5 132.4 %copy-start.36 = (bf16[16,8,8,128]{3,2,1,0:T(8,128)(2,1)}, bf16[16,8,8,128]{3,2,1,0:T(8,128)(2,1)S(1)}, u32[]{:S(2)}) copy-start(bf16[16,8,8,128]{3,2,1,0:T(8,128)(2,1)S(1)} %copy.175) | copy-start | bytes 786436
  119.3 78.8 %copy-start.28 = (bf16[128,8,64]{2,0,1:T(8,128)(2,1)}, bf16[128,8,64]{2,0,1:T(8,128)(2,1)S(1)}, u32[]{:S(2)}) copy-start(bf16[128,8,64]{2,0,1:T(8,128)(2,1)S(1)} %get-tuple-element.50) | copy-start | bytes 393220
  195.3 1.2 copy-start.7
  195.3 2.9 copy-start.39
  198.0 2.1 copy-start.20
  198.2 67.4 %copy-start.22 = (bf16[128,16,64]{2,0,1:T(8,128)(2,1)}, bf16[128,16,64]{2,0,1:T(8,128)(2,1)S(1)}, u32[]{:S(2)}) copy-start(bf16[128,16,64]{2,0,1:T(8,128)(2,1)S(1)} %copy.127) | copy-start | bytes 786436
  200.1 71.8 %copy-start.24 = (bf16[8,128,2,128]{3,1,2,0:T(8,128)(2,1)}, bf16[8,128,2,128]{3,1,2,0:T(8,128)(2,1)S(1)}, u32[]{:S(2)}) copy-start(bf16[8,128,2,128]{3,1,2,0:T(8,128)(2,1)S(1)} %convolution_convert_fusion.1) | copy-start | bytes 1572868
  265.6 7.1 copy-start.42
  271.9 426.4 %copy-start.2 = (f32[128,2048]{1,0:T(8,128)}, f32[128,2048]{1,0:T(8,128)S(1)}, u32[]{:S(2)}) copy-start(f32[128,2048]{1,0:T(8,128)S(1)} %get-tuple-element.56) | copy-start | bytes 3145732
  272.0 121.9 %copy-start.54 = (f32[128]{0:T(128)}, f32[128]{0:T(128)S(1)}, u32[]{:S(2)}) copy-start(f32[128]{0:T(128)S(1)} %add_rsqrt_fusion.2) | copy-start | bytes 1540
  272.8 251.1 %copy-start.15 = (bf16[128,2048]{1,0:T(8,128)(2,1)}, bf16[128,2048]{1,0:T(8,128)(2,1)S(1)}, u32[]{:S(2)}) copy-start(bf16[128,2048]{1,0:T(8,128)(2,1)S(1)} %multiply_convert_fusion.3) | copy-start | bytes 1572868
  407.6 246.6 %copy-start.32 = (bf16[128,2048]{1,0:T(8,128)(2,1)S(1)}, bf16[128,2048]{1,0:T(8,128)(2,1)}, u32[]{:S(2)}) copy-start(bf16[128,2048]{1,0:T(8,128)(2,1)} %param.16) | copy-start | bytes 1572868
  700.0 17.4 copy-start.4
  705.8 5.9 copy-start.10
  705.8 6.0 copy-start.43
  710.2 5.2 copy-start.21
  710.2 5.2 copy-start.23
  710.2 5.7 copy-start.29
  711.8 5.6 copy-start.25
  717.4 8.1 copy-start.30
  725.6 3.0 copy-start.45
  725.6 3.1 copy-start.56
  728.6 5.9 copy-start.8
  732.9 1.6 copy-start.35
  732.9 3.3 copy-start.40
  732.9 3.6 copy-start.41
  732.9 3.8 copy-start.33
  732.9 3.8 copy-start.52
  734.5 3.8 copy-start.17
  734.5 3.8 copy-start.49
  736.7 3.8 copy-start.47
  737.6 16.4 copy-start.26
  740.5 13.6 copy-start.18
  787.7 1.4 copy-start.13
  787.7 1841.4 %reduce-scatter.5.cloned.1.call-start = ((), (), s32[]{:S(2)}) async-start(), calls=%async_computation.10 | async-start | bytes 160432128 | tf_op jit(solution)/shard_map/reduce_scatter | solution.py:230
  789.1 32.8 %copy-start.14 = (bf16[128,6144]{1,0:T(8,128)(2,1)S(1)}, bf16[128,6144]{1,0:T(8,128)(2,1)}, u32[]{:S(2)}) copy-start(bf16[128,6144]{1,0:T(8,128)(2,1)} %get-tuple-element.26) | copy-start | bytes 4718596
  970.3 1819.6 %all-reduce.4.cloned.1.call-start = ((), (), s32[]{:S(2)}) async-start(), calls=%async_computation.11 | async-start | bytes 12582912 | tf_op jit(solution)/shard_map/psum | solution.py:290
  2635.6 1.1 copy-start.19
  2636.7 6.4 copy-start.12
  2636.7 6.4 copy-start.27
  2643.2 1.6 copy-start.1
  2643.2 2.3 copy-start.11
  2643.2 2.4 copy-start.31
  2643.2 2.3 copy-start.38
  2643.2 2.3 copy-start.48
  2645.5 2.7 copy-start.50
  2645.5 42.9 %copy-start.5 = (f32[128,2048]{1,0:T(8,128)S(1)}, f32[128,2048]{1,0:T(8,128)}, u32[]{:S(2)}) copy-start(f32[128,2048]{1,0:T(8,128)} %copy-done.4) | copy-start | bytes 3145732
  2645.5 45.5 %copy-start.3 = (f32[128,2048]{1,0:T(8,128)S(1)}, f32[128,2048]{1,0:T(8,128)}, u32[]{:S(2)}) copy-start(f32[128,2048]{1,0:T(8,128)} %copy-done.2) | copy-start | bytes 3145732
  2790.0 5.0 copy-start.6
  (6 other events, 4.9 us)
Sparse Core Ops, SparseCore 0:
  10.2 53.2 all-gather.7
  65.7 49.0 all-gather.9
  116.9 73.3 all-gather.11
  192.4 73.1 all-gather.13
  267.0 126.8 all-gather.17
  395.3 128.5 all-gather.15
  525.5 128.5 all-gather.19
  787.9 467.7 reduce-scatter.2
  1259.9 1369.1 reduce-scatter.4
  2635.8 154.1 all-reduce.3
where the time goes:
time: 2820 us; the launch traced here: 2810 us
  waiting for transfers between devices  2330 us (83%)
  matrix products  227 us (8%)
  other arithmetic  162 us (6%)
  blocking collectives  40.2 us (1%)
  local copies, waits for them, and re-layouts  28.5 us (1%)
    reduce_scatter x1, waiting for transfers between devices, on_device(): lax.psum_scatter(jnp.concatenate([contract_rows(left_in, mlp_right), cont...  1370 us
    reduce_scatter x1, waiting for transfers between devices, on_device(): lax.psum_scatter(jnp.concatenate([contract_rows(left_in, attn_right), con...  285 us
    all_gather x1, waiting for transfers between devices, on_device(): lax.all_gather(w_up, 'shard', axis=0, tiled=True)  121 us
    all_gather x1, waiting for transfers between devices, on_device(): lax.all_gather(w_down, 'shard', axis=0, tiled=True)  117 us
    all_gather x1, waiting for transfers between devices, on_device(): lax.all_gather(w_gate, 'shard', axis=0, tiled=True)  116 us
    dot_general x4, matrix products, contract_rows(): lax.dot_general(left, right, (((0,), (0,)), ((), ())), preferred_element_...  103 us
    concatenate x1, other arithmetic, on_device(): jnp.concatenate([contract_rows(left_in, mlp_right), contract_rows(left_gr...  100 us
    psum x1, waiting for transfers between devices, on_device(): lax.psum(attn_grads.astype(jnp.bfloat16), 'rep').astype(jnp.float32)  84.7 us
  transfers between devices with their start and end apart: 10, of which 10 were waited for; matrix products, arithmetic and copies ran while one was open for 9% of the time, Pallas kernels for 0%

commit v1 on v0

--- a/solution.py
+++ b/solution.py
@@ -7,6 +7,18 @@
 EPSILON = 1e-06
 ROPE_BASE = 1000000.0
 NEG_FILL = -1e30
+
+
+def doubled_up(value, axis, dim):
+    ways, here, lap = (lax.axis_size(axis), lax.axis_index(axis), value.shape[dim])
+    line, have = (value, 1)
+    while have < ways:
+        line = jnp.concatenate(
+            [line, lax.ppermute(line, axis, [(d, (d - have) % ways) for d in range(ways)])],
+            axis=dim,
+        )
+        have = 2 * have
+    return jnp.roll(line, here * lap, axis=dim)
 
 
 def rope_tables(positions, half):
@@ -193,7 +205,7 @@
     attended_rows, log_total = attend_forward(
         rotated_query_rows, rotated_key_rows, value_rows, mask
     )
-    attn_out = contract_cols(attended_rows, lax.all_gather(w_o, "shard", axis=0, tiled=True))
+    attn_out = contract_cols(attended_rows, doubled_up(w_o, "shard", 0))
     mid = inputs + attn_out
     recip_mlp = lax.rsqrt(jnp.mean(mid * mid, -1, keepdims=True) + EPSILON)
     mlp_in = (mid * recip_mlp * mlp_gain).astype(jnp.bfloat16)

time: 2820 us -> 3000 us (1.064)
  waiting for transfers between devices: 2330 us -> 2480 us
    all_gather x1, waiting for transfers between devices: 48.2 us -> 208 us  [on_device(): lax.all_gather(key_matrix, 'shard', axis=0, tiled=True)]
    ppermute x0 -> x4, waiting for transfers between devices: none -> 98.4 us  [doubled_up(): lax.ppermute(line, axis, [(d, (d - have) % ways) for d in range(ways)])]
    all_gather x1, waiting for transfers between devices: 49.1 us -> 0.01 us  [on_device(): lax.all_gather(value_matrix, 'shard', axis=0, tiled=True)]
    all_gather x1, waiting for transfers between devices: 65.4 us -> 30.4 us  [on_device(): lax.all_gather(w_o, 'shard', axis=0, tiled=True)]
  transfers between devices with their start and end apart: 10 -> 14, of which waited for: 10 -> 12; matrix products, arithmetic and copies ran while one was open for 9% -> 11% of each run, Pallas kernels for 0% -> 0%
where the time goes in v1:
time: 3000 us; the launch traced here: 2990 us
  waiting for transfers between devices  2480 us (83%)
  matrix products  227 us (8%)
  other arithmetic  163 us (5%)
  local copies, waits for them, and re-layouts  49.1 us (2%)
  blocking collectives  40.2 us (1%)
    reduce_scatter x1, waiting for transfers between devices, on_device(): lax.psum_scatter(jnp.concatenate([contract_rows(left_in, mlp_right), cont...  1370 us
    reduce_scatter x1, waiting for transfers between devices, on_device(): lax.psum_scatter(jnp.concatenate([contract_rows(left_in, attn_right), con...  284 us
    all_gather x1, waiting for transfers between devices, on_device(): lax.all_gather(key_matrix, 'shard', axis=0, tiled=True)  208 us
    all_gather x1, waiting for transfers between devices, on_device(): lax.all_gather(w_down, 'shard', axis=0, tiled=True)  117 us
    all_gather x1, waiting for transfers between devices, on_device(): lax.all_gather(w_gate, 'shard', axis=0, tiled=True)  116 us
    all_gather x1, waiting for transfers between devices, on_device(): lax.all_gather(w_up, 'shard', axis=0, tiled=True)  112 us
    dot_general x4, matrix products, contract_rows(): lax.dot_general(left, right, (((0,), (0,)), ((), ())), preferred_element_...  102 us
    concatenate x1, other arithmetic, on_device(): jnp.concatenate([contract_rows(left_in, mlp_right), contract_rows(left_gr...  99.9 us
  transfers between devices with their start and end apart: 14, of which 12 were waited for; matrix products, arithmetic and copies ran while one was open for 11% of the time, Pallas kernels for 0%

profile of v1, /device:TPU:0, one launch (start us, length us, event | category | flops | bytes accessed | tf_op | source)
XLA Modules:
  0.0 2987.3 jit_solution(10173627016063646277)
XLA Ops:
  11.2 5.5 collective-permute-start
  16.7 10.1 collective-permute-done
  26.9 25.7 collective-permute-done.1
  52.9 2.8 collective-permute-start.2
  55.7 62.7 %collective-permute-done.2 = bf16[512,2048]{1,0:T(8,128)(2,1)S(1)} collective-permute-done((bf16[512,2048]{1,0:T(8,128)(2,1)S(1)}, bf16[512,2048]{1,0:T(8,128)(2,1)S(1)}, u32[]{:S(2)}, u32[]{:S(2)}) %collective-permute-start.2) | collective-permute-done | bytes 2097184 | tf_op jit(solution)/shard_map/ppermute | solution.py:17
  118.4 2.3 pad_maximum_fusion.2
  120.7 1.6 collective-permute-start.3
  124.9 1.9 constant_dynamic-update-slice_fusion.9
  126.7 1.9 constant_dynamic-update-slice_fusion.8
  128.6 2.4 constant_dynamic-update-slice_fusion.7
  131.0 1.5 constant_dynamic-update-slice_fusion.6
  132.5 3.0 fusion.24
  136.2 208.3 %all-gather.10.cloned.1.call-done = bf16[2048,1024]{1,0:T(8,128)(2,1)} async-done(((bf16[128,1024]{1,0:T(8,128)(2,1)}), bf16[2048,1024]{1,0:T(8,128)(2,1)}) %all-gather.10.cloned.1.call-update) | async-done | bytes 4194320 | tf_op jit(solution)/shard_map/all_gather | solution.py:188
  344.6 2.9 fusion.72
  349.4 4.9 constant_dynamic-update-slice_fusion.5
  356.0 1.1 constant_dynamic-update-slice_fusion.2
  357.6 1.5 constant_dynamic-update-slice_fusion.1
  359.1 4.8 constant_dynamic-update-slice_fusion
  363.8 56.4 %all-gather.12.cloned.1.call-done = bf16[2048,2048]{1,0:T(8,128)(2,1)} async-done(((bf16[128,2048]{1,0:T(8,128)(2,1)}), bf16[2048,2048]{1,0:T(8,128)(2,1)}) %all-gather.12.cloned.1.call-update) | async-done | bytes 8388624 | tf_op jit(solution)/shard_map/all_gather | solution.py:187
  420.2 4.7 fusion.70
  429.1 6.6 multiply_reduce_fusion.4
  436.6 111.9 %all-gather.16.cloned.1.call-done = bf16[2048,6144]{1,0:T(8,128)(2,1)} async-done(((bf16[128,6144]{1,0:T(8,128)(2,1)}), bf16[2048,6144]{1,0:T(8,128)(2,1)}) %all-gather.16.cloned.1.call-update) | async-done | bytes 25165840 | tf_op jit(solution)/shard_map/all_gather | solution.py:214
  548.5 13.7 fusion.81
  562.1 116.4 %all-gather.14.cloned.1.call-done = bf16[2048,6144]{1,0:T(8,128)(2,1)} async-done(((bf16[128,6144]{1,0:T(8,128)(2,1)}), bf16[2048,6144]{1,0:T(8,128)(2,1)}) %all-gather.14.cloned.1.call-update) | async-done | bytes 25165840 | tf_op jit(solution)/shard_map/all_gather | solution.py:213
  678.5 13.3 fusion.80
  691.8 116.8 %all-gather.18.cloned.1.call-done = bf16[2048,6144]{1,0:T(8,128)(2,1)} async-done(((bf16[128,6144]{1,0:T(8,128)(2,1)}), bf16[2048,6144]{1,0:T(8,128)(2,1)}) %all-gather.18.cloned.1.call-update) | async-done | bytes 25165840 | tf_op jit(solution)/shard_map/all_gather | solution.py:222
  808.6 14.6 multiply_convert_fusion
  823.3 14.7 fusion.82
  837.9 15.7 multiply_reduce_fusion
  853.7 1.6 multiply_add_fusion.1
  855.3 30.4 %all-gather.20.cloned.1.call-done = bf16[2048,2048]{1,0:T(8,128)(2,1)} async-done(((bf16[128,2048]{1,0:T(8,128)(2,1)}), bf16[2048,2048]{1,0:T(8,128)(2,1)}) %all-gather.20.cloned.1.call-update) | async-done | bytes 8388624 | tf_op jit(solution)/shard_map/all_gather | solution.py:254
  885.7 4.6 convolution_convert_fusion
  891.3 1.2 copy.132
  892.5 1.6 multiply_reduce_fusion.2
  894.1 1.4 fusion.23
  895.6 1.6 fusion.20
  897.7 1.5 convolution_multiply_fusion
  899.2 8.2 fusion.55
  907.5 2.1 fusion.78
  910.4 1.1 fusion.60
  912.3 2.4 copy.169
  914.7 1.5 multiply_add_fusion
  916.3 1.6 multiply_reduce_fusion.1
  920.0 2.2 fusion.35
  923.0 13.5 fusion.36
  936.6 33.6 %pad_maximum_fusion.1 = f32[2048,6144]{1,0:T(8,128)} fusion(f32[2048,2048]{1,0:T(8,128)} %fusion.55, f32[2048,4096]{1,0:T(8,128)} %fusion.36), kind=kLoop, calls=%fused_computation.1 | loop fusion | flops 12582912 | bytes 100663296 | tf_op jit(solution)/shard_map/concatenate | solution.py:289
  970.3 1.3 copy-done.21
  971.6 33.9 %convolution_bitcast_fusion = f32[2048,6144]{1,0:T(8,128)} fusion(bf16[128,6144]{1,0:T(8,128)(2,1)S(1)} %copy-done.21, bf16[128,2048]{1,0:T(8,128)(2,1)} %param.16), kind=kOutput, calls=%fused_computation.2 | convolution fusion | flops 3221225472 | bytes 52428800 | tf_op jit(solution)/shard_map/dot_general | solution.py:64
  1005.5 46.9 %fusion.2 = f32[2048,12288]{1,0:T(8,128)} fusion(bf16[128,2048]{1,0:T(8,128)(2,1)} %copy-done.24, bf16[128,6144]{1,0:T(8,128)(2,1)} %get-tuple-element.25, bf16[128,6144]{1,0:T(8,128)(2,1)S(1)} %copy-done.23), kind=kOutput, calls=%fused_computation.6 | convolution fusion | flops 6448742400 | bytes 104333312 | tf_op jit(solution)/shard_map/dot_general | solution.py:64
  1052.3 99.9 %pad_maximum_fusion = f32[2048,18432]{1,0:T(8,128)} fusion(f32[2048,6144]{1,0:T(8,128)} %convolution_bitcast_fusion, f32[2048,12288]{1,0:T(8,128)} %fusion.2), kind=kLoop, calls=%fused_computation | loop fusion | flops 37748736 | bytes 301989888 | tf_op jit(solution)/shard_map/concatenate | solution.py:243
  1152.6 284.0 %reduce-scatter.3.cloned.1.call-done = f32[128,6144]{1,0:T(8,128)} async-done(((f32[2048,6144]{1,0:T(8,128)}), f32[128,6144]{1,0:T(8,128)}) %reduce-scatter.3.cloned.1.call-update) | async-done | bytes 3145744 | tf_op jit(solution)/shard_map/reduce_scatter | solution.py:288
  1436.6 3.2 convert_element_type.156
  1439.8 1370.4 %reduce-scatter.5.cloned.1.call-done = f32[128,18432]{1,0:T(8,128)} async-done(((f32[2048,18432]{1,0:T(8,128)}), f32[128,18432]{1,0:T(8,128)}) %reduce-scatter.5.cloned.1.call-update) | async-done | bytes 9437200 | tf_op jit(solution)/shard_map/reduce_scatter | solution.py:242
  2810.2 6.5 convert_element_type.158
  2817.7 6.4 fusion.83
  2824.2 1.5 convolution_add_fusion.1
  2826.6 2.7 fusion.30
  2829.3 40.2 %all-reduce = (f32[2048]{0:T(1024)}, f32[2048]{0:T(1024)}, f32[128]{0:T(128)}, f32[128]{0:T(128)}) all-reduce(f32[2048]{0:T(1024)S(1)} %get-tuple-element.15, f32[2048]{0:T(1024)S(1)} %copy-done.59, f32[128]{0:T(128)S(1)} %bitcast_reduce_fusion, f32[128]{0:T(128)S(1)} %bitcast_reduce_fusion.1), channel_id=1, replica_groups=mesh['rep'=2,'shard'=16] {'rep','shard'}, use_global_device_ids=true, to_apply=%region_16.17 | all-reduce | flops 4352 | bytes 34816 | tf_op jit(solution)/shard_map/psum | solution.py:298
  2869.5 2.6 fusion.29
  2872.0 14.2 fusion.10
  2886.2 84.7 %all-reduce.4.cloned.1.call-done = (bf16[128,6144]{1,0:T(8,128)(2,1)}, bf16[128,18432]{1,0:T(8,128)(2,1)}) async-done(((bf16[128,6144]{1,0:T(8,128)(2,1)}, bf16[128,18432]{1,0:T(8,128)(2,1)}), (bf16[128,6144]{1,0:T(8,128)(2,1)}, bf16[128,18432]{1,0:T(8,128)(2,1)})) %all-reduce.4.cloned.1.call-update) | async-done | bytes 6291472 | tf_op jit(solution)/shard_map/psum | solution.py:302
  2971.0 2.3 fusion.77
  2973.2 2.8 fusion.76
  2976.0 4.0 fusion.75
  (212 shorter events, 24.7 us)
Async XLA Ops:
  7.2 4.0 copy-start.7
  7.2 125.3 %all-gather.8.cloned.1.call-start = ((), (), s32[]{:S(2)}) async-start(), calls=%async_computation.2 | async-start | bytes 4456448 | tf_op jit(solution)/shard_map/all_gather | solution.py:189
  7.9 336.6 %all-gather.10.cloned.1.call-start = ((), (), s32[]{:S(2)}) async-start(), calls=%async_computation.3 | async-start | bytes 4456448 | tf_op jit(solution)/shard_map/all_gather | solution.py:188
  8.7 411.5 %all-gather.12.cloned.1.call-start = ((), (), s32[]{:S(2)}) async-start(), calls=%async_computation.4 | async-start | bytes 8912896 | tf_op jit(solution)/shard_map/all_gather | solution.py:187
  9.4 539.1 %all-gather.16.cloned.1.call-start = ((), (), s32[]{:S(2)}) async-start(), calls=%async_computation.6 | async-start | bytes 26738688 | tf_op jit(solution)/shard_map/all_gather | solution.py:214
  10.0 668.6 %all-gather.14.cloned.1.call-start = ((), (), s32[]{:S(2)}) async-start(), calls=%async_computation.5 | async-start | bytes 26738688 | tf_op jit(solution)/shard_map/all_gather | solution.py:213
  10.6 798.0 %all-gather.18.cloned.1.call-start = ((), (), s32[]{:S(2)}) async-start(), calls=%async_computation.7 | async-start | bytes 26738688 | tf_op jit(solution)/shard_map/all_gather | solution.py:222
  11.1 874.5 %all-gather.20.cloned.1.call-start = ((), (), s32[]{:S(2)}) async-start(), calls=%async_computation.8 | async-start | bytes 8912896 | tf_op jit(solution)/shard_map/all_gather | solution.py:254
  11.2 15.6 collective-permute-start
  26.8 93.9 %copy-start.19 = (bf16[128,2048]{1,0:T(8,128)(2,1)}, bf16[128,2048]{1,0:T(8,128)(2,1)S(1)}, u32[]{:S(2)}) copy-start(bf16[128,2048]{1,0:T(8,128)(2,1)S(1)} %collective-permute-done) | copy-start | bytes 1572868
  26.8 25.8 collective-permute-start.1
  52.6 68.1 %copy-start.14 = (bf16[256,2048]{1,0:T(8,128)(2,1)}, bf16[256,2048]{1,0:T(8,128)(2,1)S(1)}, u32[]{:S(2)}) copy-start(bf16[256,2048]{1,0:T(8,128)(2,1)S(1)} %collective-permute-done.1) | copy-start | bytes 3145732
  52.9 69.6 %copy-start = (bf16[128,2048]{1,0:T(8,128)(2,1)S(1)}, bf16[128,2048]{1,0:T(8,128)(2,1)}, u32[]{:S(2)}) copy-start(bf16[128,2048]{1,0:T(8,128)(2,1)} %param.15) | copy-start | bytes 1572868
  52.9 69.7 %copy-start.69 = (s32[1,128]{1,0:T(1,128)S(1)}, s32[1,128]{1,0:T(1,128)}, u32[]{:S(2)}) copy-start(s32[1,128]{1,0:T(1,128)} %param.18) | copy-start | bytes 1540
  52.9 69.8 %copy-start.64 = (f32[128]{0:T(128)S(1)}, f32[128]{0:T(128)}, u32[]{:S(2)}) copy-start(f32[128]{0:T(128)} %param.22) | copy-start | bytes 1540
  52.9 70.4 %copy-start.66 = (f32[128]{0:T(128)S(1)}, f32[128]{0:T(128)}, u32[]{:S(2)}) copy-start(f32[128]{0:T(128)} %param.21) | copy-start | bytes 1540
  52.9 71.0 %copy-start.68 = (s32[1,128]{1,0:T(1,128)S(1)}, s32[1,128]{1,0:T(1,128)}, u32[]{:S(2)}) copy-start(s32[1,128]{1,0:T(1,128)} %param.17) | copy-start | bytes 1540
  52.9 65.5 %collective-permute-start.2 = (bf16[512,2048]{1,0:T(8,128)(2,1)S(1)}, bf16[512,2048]{1,0:T(8,128)(2,1)S(1)}, u32[]{:S(2)}, u32[]{:S(2)}) collective-permute-start(bf16[512,2048]{1,0:T(8,128)(2,1)S(1)} %pad_maximum_fusion.3), channel_id=1, source_target_pairs={{0,12},{1,13},{2,14},{3,15},{4,0},{5,1},{6,2},{7,3},{8,4},{9,5},{1... | collective-permute-start | bytes 6291464 | tf_op jit(solution)/shard_map/ppermute | solution.py:17
  120.7 228.8 %collective-permute-start.3 = (bf16[1024,2048]{1,0:T(8,128)(2,1)}, bf16[1024,2048]{1,0:T(8,128)(2,1)}, u32[]{:S(2)}, u32[]{:S(2)}) collective-permute-start(bf16[1024,2048]{1,0:T(8,128)(2,1)} %pad_maximum_fusion.2), channel_id=1, source_target_pairs={{0,8},{1,9},{2,10},{3,11},{4,12},{5,13},{6,14},{7,15},{8,0},{9,1},... | collective-permute-start | bytes 12582920 | tf_op jit(solution)/shard_map/ppermute | solution.py:17
  122.3 1314.2 %reduce-scatter.3.cloned.1.call-start = ((), (), s32[]{:S(2)}) async-start(), calls=%async_computation.9 | async-start | bytes 53477376 | tf_op jit(solution)/shard_map/reduce_scatter | solution.py:288
  122.7 297.5 %copy-start.55 = (f32[128]{0:T(128)}, f32[128]{0:T(128)S(1)}, u32[]{:S(2)}) copy-start(f32[128]{0:T(128)S(1)} %add_rsqrt_fusion.3) | copy-start | bytes 1540
  124.9 7.7 copy-start.46
  348.7 8.4 copy-start.53
  349.4 5.7 copy-start.20
  349.4 6.6 copy-start.15
  354.3 2.8 copy-start.17
  357.6 69.9 %copy-start.37 = (bf16[128,8,64]{2,0,1:T(8,128)(2,1)}, bf16[128,8,64]{2,0,1:T(8,128)(2,1)S(1)}, u32[]{:S(2)}) copy-start(bf16[128,8,64]{2,0,1:T(8,128)(2,1)S(1)} %get-tuple-element.50) | copy-start | bytes 393220
  363.8 62.4 %copy-start.67 = (f32[128]{0:T(128)S(1)}, f32[128]{0:T(128)}, u32[]{:S(2)}) copy-start(f32[128]{0:T(128)} %param.21) | copy-start | bytes 1540
  429.1 6.6 copy-start.33
  429.1 7.3 copy-start.51
  435.7 418.0 %copy-start.2 = (f32[128,2048]{1,0:T(8,128)}, f32[128,2048]{1,0:T(8,128)S(1)}, u32[]{:S(2)}) copy-start(f32[128,2048]{1,0:T(8,128)S(1)} %get-tuple-element.56) | copy-start | bytes 3145732
  435.7 126.4 %copy-start.63 = (f32[128]{0:T(128)}, f32[128]{0:T(128)S(1)}, u32[]{:S(2)}) copy-start(f32[128]{0:T(128)S(1)} %add_rsqrt_fusion.2) | copy-start | bytes 1540
  436.5 242.0 %copy-start.24 = (bf16[128,2048]{1,0:T(8,128)(2,1)}, bf16[128,2048]{1,0:T(8,128)(2,1)S(1)}, u32[]{:S(2)}) copy-start(bf16[128,2048]{1,0:T(8,128)(2,1)S(1)} %multiply_convert_fusion.3) | copy-start | bytes 1572868
  823.3 14.7 copy-start.22
  837.9 15.7 copy-start.41
  855.3 43.9 %copy-start.4 = (f32[128,2048]{1,0:T(8,128)}, f32[128,2048]{1,0:T(8,128)S(1)}, u32[]{:S(2)}) copy-start(f32[128,2048]{1,0:T(8,128)S(1)} %multiply_add_fusion.1) | copy-start | bytes 3145732
  890.3 3.8 copy-start.11
  890.3 3.8 copy-start.52
  892.5 4.6 copy-start.30
  892.5 4.7 copy-start.32
  892.5 5.1 copy-start.38
  894.1 5.0 copy-start.34
  895.6 11.8 copy-start.39
  907.3 3.1 copy-start.18
  907.3 3.1 copy-start.54
  907.3 3.1 copy-start.65
  910.4 5.9 copy-start.9
  914.7 3.3 copy-start.49
  914.7 3.5 copy-start.50
  914.7 3.7 copy-start.42
  914.7 3.7 copy-start.61
  916.3 3.7 copy-start.26
  916.3 3.7 copy-start.58
  918.4 4.7 copy-start.56
  919.3 17.3 copy-start.35
  970.2 1840.0 %reduce-scatter.5.cloned.1.call-start = ((), (), s32[]{:S(2)}) async-start(), calls=%async_computation.10 | async-start | bytes 160432128 | tf_op jit(solution)/shard_map/reduce_scatter | solution.py:242
  971.6 33.9 %copy-start.23 = (bf16[128,6144]{1,0:T(8,128)(2,1)S(1)}, bf16[128,6144]{1,0:T(8,128)(2,1)}, u32[]{:S(2)}) copy-start(bf16[128,6144]{1,0:T(8,128)(2,1)} %copy-done.22) | copy-start | bytes 4718596
  1152.3 1818.7 %all-reduce.4.cloned.1.call-start = ((), (), s32[]{:S(2)}) async-start(), calls=%async_computation.11 | async-start | bytes 12582912 | tf_op jit(solution)/shard_map/psum | solution.py:302
  2817.7 6.4 copy-start.13
  2817.7 6.4 copy-start.36
  2826.6 2.7 copy-start.59
  2826.6 42.9 %copy-start.5 = (f32[128,2048]{1,0:T(8,128)S(1)}, f32[128,2048]{1,0:T(8,128)}, u32[]{:S(2)}) copy-start(f32[128,2048]{1,0:T(8,128)} %copy-done.4) | copy-start | bytes 3145732
  2826.6 45.5 %copy-start.3 = (f32[128,2048]{1,0:T(8,128)S(1)}, f32[128,2048]{1,0:T(8,128)}, u32[]{:S(2)}) copy-start(f32[128,2048]{1,0:T(8,128)} %copy-done.2) | copy-start | bytes 3145732
  2971.0 5.0 copy-start.6
  (20 other events, 30.9 us)
Sparse Core Ops, SparseCore 0:
  10.2 85.4 all-gather.7
  97.9 246.6 all-gather.9
  346.7 73.3 all-gather.11
  421.6 126.8 all-gather.15
  549.9 128.5 all-gather.13
  680.0 128.5 all-gather.17
  810.8 74.8 all-gather.19
  970.4 466.1 reduce-scatter.2
  1440.8 1369.3 reduce-scatter.4
  2816.8 154.1 all-reduce.3
